TPU v7x, 32 devices: a whole 2x2x4 slice. The times are simulated.
32 devices in a mesh: ctx: 8 (over y, x, core), page: 4 (over z).
Axes of the slice: x: 2, y: 2, z: 4, core: 2. Of those that a mesh axis runs over, the one named last changes fastest.
Arguments:
- queries: bfloat16 [2048, 8192], P('ctx', 'page'), may hold values from -200 to 200
- keys: bfloat16 [2048, 512], P('ctx', 'page'), may hold values from -6 to 6
- values: bfloat16 [2048, 512], P('ctx', 'page'), may hold values from -6 to 6
- span_table: int32 [16], replicated, may hold values from 0 to 15, each once
- page_slots: int32 [16], replicated, may hold values from 0 to 15, each once
Outputs:
- attended: bfloat16 [2048, 8192], P('ctx', 'page')
- cache_pages: bfloat16 [16, 4, 2, 128, 128], P('ctx')
- cache_scales: float32 [16, 4, 2], P('ctx')
Inputs may be any that keep to these rules, and one draw needn't show every extreme that they name: Stored span i (rows i * 128 to (i + 1) * 128 - 1) holds prompt positions span_table[i] * 128 onward; every value appears once. `page_slots`: every slot is named by exactly one page.
All inputs are finite; a program needn't handle non-finite values. Where the computation divides by a largest or mean magnitude, that divisor is 1e-20 or more.
Results may differ from a plain program's by a relative error of at most 0.0055.
Values may be sent and summed in bfloat16 or wider, within the bound.
A program may use at most 64 MiB of HBM per device.

v0:
```python
import math

import jax
import jax.numpy as jnp
from jax import lax
from jax.sharding import PartitionSpec as P

DH = 128
PAGE = 128
SPAN = 128


def on_device(queries, keys, values, span_table, page_slots):
    rows = queries.shape[0]
    kv_here = keys.shape[1] // DH
    q_here = queries.shape[1] // DH
    group = q_here // kv_here
    ctx_index = lax.axis_index("ctx")
    table_size = span_table.shape[0]
    scale = DH ** (-0.5)

    def token_positions(start, count):
        span_ids = start // SPAN + jnp.arange(count // SPAN, dtype=jnp.int32)
        onehot = span_ids[:, None] == jnp.arange(table_size, dtype=jnp.int32)[None, :]
        placed = jnp.sum(jnp.where(onehot, span_table[None, :], 0), axis=1)
        inner = jnp.arange(SPAN, dtype=jnp.int32)
        return (placed[:, None] * SPAN + inner[None, :]).reshape(count)

    query_pos = token_positions(ctx_index * rows, rows)
    query_heads = queries.reshape(rows, kv_here, group, DH)
    slots_here = rows // PAGE
    first_slot = ctx_index * slots_here
    page_ids = jnp.arange(page_slots.shape[0], dtype=jnp.int32)
    wanted = [
        jnp.sum(jnp.where(page_slots == first_slot + j, page_ids, 0)) for j in range(slots_here)
    ]

    def collect(held, piece):
        count = piece.shape[0]
        updated = []
        for j in range(slots_here):
            offset = wanted[j] * PAGE
            inside = (offset >= 0) & (offset + PAGE <= count)
            clamped = jnp.clip(offset, 0, count - PAGE)
            picked = lax.dynamic_slice_in_dim(piece, clamped, PAGE, 0)
            updated.append(jnp.where(inside, picked, held[j]))
        return jnp.stack(updated, axis=0)

    start_state = (
        jnp.full((kv_here, group, rows), -1e30, jnp.float32),
        jnp.zeros((kv_here, group, rows), jnp.float32),
        jnp.zeros((kv_here, group, rows, DH), jnp.float32),
    )
    empty_pages = jnp.zeros((slots_here, PAGE, kv_here * DH), jnp.bfloat16)
    state = start_state
    key_pages = empty_pages
    value_pages = empty_pages
    key_piece = lax.all_gather(keys, "ctx", axis=0, tiled=True)
    value_piece = lax.all_gather(values, "ctx", axis=0, tiled=True)
    count = key_piece.shape[0]
    key_pos = token_positions(jnp.int32(0), count)
    attend_state = state
    attend_key_piece = key_piece.reshape(count, kv_here, DH)
    attend_value_piece = value_piece.reshape(count, kv_here, DH)
    attend_count = attend_key_piece.shape[0]
    width = math.gcd(attend_count, 512)
    blocks = attend_count // width
    key_blocks = attend_key_piece.reshape(blocks, width, kv_here, DH)
    value_blocks = attend_value_piece.reshape(blocks, width, kv_here, DH)
    pos_blocks = key_pos.reshape(blocks, width)

    def step(carry, block):
        top, total, summed = carry
        key_block, value_block, pos_block = block
        score = (
            jnp.einsum("qhgd,khd->hgqk", query_heads, key_block, preferred_element_type=jnp.float32)
            * scale
        )
        keep = pos_block[None, :] <= query_pos[:, None]
        score = jnp.where(keep[None, None], score, -1e30)
        new_top = jnp.maximum(top, jnp.max(score, axis=-1))
        factor = jnp.exp(top - new_top)
        weight = jnp.where(keep[None, None], jnp.exp(score - new_top[..., None]), 0.0)
        total = total * factor + jnp.sum(weight, axis=-1)
        update = jnp.einsum(
            "hgqk,khd->hgqd",
            weight.astype(jnp.bfloat16),
            value_block,
            preferred_element_type=jnp.float32,
        )
        summed = summed * factor[..., None] + update
        return ((new_top, total, summed), None)

    attend_state, unused = lax.scan(step, attend_state, (key_blocks, value_blocks, pos_blocks))
    state = attend_state
    state, key_pages, value_pages = (
        state,
        collect(key_pages, key_piece),
        collect(value_pages, value_piece),
    )
    key_pages = key_pages.reshape(slots_here, PAGE, kv_here, DH).transpose(0, 2, 1, 3)
    value_pages = value_pages.reshape(slots_here, PAGE, kv_here, DH).transpose(0, 2, 1, 3)
    local_raw = jnp.stack([key_pages, value_pages], axis=2)
    raw = lax.all_gather(local_raw, "page", axis=1, tiled=True)
    top, total, summed = state
    result = summed / total[..., None]
    attended = jnp.transpose(result, (2, 0, 1, 3)).reshape(rows, q_here * DH).astype(jnp.bfloat16)
    raw_float = raw.astype(jnp.float32)
    cache_scales = jnp.max(jnp.abs(raw_float), axis=(3, 4)) + 1e-06
    cache_pages = (raw_float / cache_scales[..., None, None]).astype(jnp.bfloat16)
    return (attended, cache_pages, cache_scales)


def solution(mesh):
    placed = (P("ctx", "page"), P("ctx", "page"), P("ctx", "page"), P(), P())
    return jax.shard_map(
        on_device,
        mesh=mesh,
        in_specs=placed,
        out_specs=(P("ctx", "page"), P("ctx", None, None, None, None), P("ctx", None, None)),
        check_vma=False,
    )
```

profile of v0, /device:TPU:1, one launch (start us, length us, event | category | flops | bytes accessed | tf_op | source)
XLA Modules:
  0.0 110.0 jit_solution(16091338165210521844)
XLA Ops:
  0.7 0.8 select_reduce_fusion
  1.6 11.5 %all_gather.9 = bf16[2048,128]{1,0:T(8,128)(2,1)S(1)} all-gather(bf16[256,128]{1,0:T(8,128)(2,1)} %param.8), channel_id=1, replica_groups=mesh['ctx'=8,'page'=4] {'ctx'}, dimensions={0}, use_global_device_ids=true | all-gather | bytes 589824 | tf_op jit(solution)/shard_map/all_gather | solution.py:58
  13.1 1.5 %copy.31 = bf16[256,2048]{0,1:T(8,128)(2,1)S(1)} copy(bf16[256,2048]{1,0:T(8,128)(2,1)} %param.7) | data formatting | bytes 2097152 | tf_op args[0]
  14.6 0.7 copy.33
  15.3 9.5 %all_gather.10 = bf16[2048,128]{1,0:T(8,128)(2,1)S(1)} all-gather(bf16[256,128]{1,0:T(8,128)(2,1)} %param.9), channel_id=1, replica_groups=mesh['ctx'=8,'page'=4] {'ctx'}, dimensions={0}, use_global_device_ids=true | all-gather | bytes 589824 | tf_op jit(solution)/shard_map/all_gather | solution.py:59
  24.8 0.8 fusion.26
  25.6 61.7 %while.15 = (s32[]{:T(128)}, f32[1,16,256]{2,1,0:T(8,128)S(1)}, f32[1,16,256]{2,1,0:T(8,128)S(1)}, f32[1,16,256,128]{3,2,1,0:T(8,128)}, s32[4,512]{1,0:T(4,128)S...) while((s32[]{:T(128)}, f32[1,16,256]{2,1,0:T(8,128)S(1)}, ...), condition=%wide.region_5.6_spmd.clone, body=%wide.region_2.5_spmd.clone.sunk | while | flops 1102733568 | bytes 65020080 | solution.py:94
  25.7 0.1 broadcast_compare_fusion.2
  25.9 4.6 %fusion.36 = (f32[16,256]{1,0:T(8,128)S(1)}, f32[512,256,16]{1,0,2:T(8,128)}) fusion(pred[256,512]{0,1:T(8,128)(4,1)S(1)} %broadcast_compare_fusion.2, bf16[256,1,16,128]{3,0,2,1:T(8,128)(2,1)S(1)} %get-tuple-element.249, bf16[4,512,1,128]{3,1,2,0:T(8,128)(2,1)S(1)} %get-tuple-element.248, s32[]{:T(128)S(6)} %copy.48), kind=kOutput, calls=%fused_computation.3.clone.1 | convolution fusion | flops 543158272 | bytes 9715716 | tf_op jit(solution)/shard_map/while/body/eval_jaxpr/qhgd,khd->hgqk/dot_general | solution.py:76
  30.5 4.6 %fusion.38 = f32[16,256]{1,0:T(8,128)S(1)} fusion(f32[512,256,16]{1,0,2:T(8,128)} %get-tuple-element.219, f32[16,256]{1,0:T(8,128)S(1)} %bitcast.114, pred[256,512]{0,1:T(8,128)(4,1)S(1)} %broadcast_compare_fusion.2), kind=kLoop, calls=%fused_computation.5.clone.1 | loop fusion | flops 10481664 | bytes 8552448 | tf_op jit(solution)/shard_map/while/body/eval_jaxpr/reduce_sum | solution.py:84
  35.1 1.2 %copy-done = f32[512,256,16]{1,0,2:T(8,128)S(1)} copy-done((f32[512,256,16]{1,0,2:T(8,128)S(1)}, f32[512,256,16]{1,0,2:T(8,128)}, u32[]{:S(2)}) %copy-start) | copy-done | bytes 8388632 | tf_op jit(solution)/shard_map/while
  36.3 3.9 %bitcast_add_fusion.6 = f32[1,16,256,128]{3,2,1,0:T(8,128)} fusion(f32[1,16,256,128]{3,2,1,0:T(8,128)} %get-tuple-element.235, f32[512,256,16]{1,0,2:T(8,128)S(1)} %copy-done, f32[16,256]{1,0:T(8,128)S(1)} %bitcast.115, pred[256,512]{0,1:T(8,128)(4,1)S(1)} %broadcast_compare_fusion.2, f32[16,256]{1,0:T(8,128)S(1)} %get-tuple-element.220, ...), kind=kOutput, calls=%fused_computation.9.clone.1 | convolution fusion | flops 548929536 | bytes 12877829 | tf_op jit(solution)/shard_map/while/body/eval_jaxpr/hgqk,khd->hgqd/dot_general | solution.py:85
  40.4 4.6 %fusion.36 = (f32[16,256]{1,0:T(8,128)S(1)}, f32[512,256,16]{1,0,2:T(8,128)}) fusion(pred[256,512]{0,1:T(8,128)(4,1)S(1)} %broadcast_compare_fusion.2, bf16[256,1,16,128]{3,0,2,1:T(8,128)(2,1)S(1)} %get-tuple-element.249, bf16[4,512,1,128]{3,1,2,0:T(8,128)(2,1)S(1)} %get-tuple-element.248, s32[]{:T(128)S(6)} %copy.48), kind=kOutput, calls=%fused_computation.3.clone.1 | convolution fusion | flops 543158272 | bytes 9715716 | tf_op jit(solution)/shard_map/while/body/eval_jaxpr/qhgd,khd->hgqk/dot_general | solution.py:76
  45.0 4.6 %fusion.38 = f32[16,256]{1,0:T(8,128)S(1)} fusion(f32[512,256,16]{1,0,2:T(8,128)} %get-tuple-element.219, f32[16,256]{1,0:T(8,128)S(1)} %bitcast.114, pred[256,512]{0,1:T(8,128)(4,1)S(1)} %broadcast_compare_fusion.2), kind=kLoop, calls=%fused_computation.5.clone.1 | loop fusion | flops 10481664 | bytes 8552448 | tf_op jit(solution)/shard_map/while/body/eval_jaxpr/reduce_sum | solution.py:84
  49.6 1.2 %copy-done = f32[512,256,16]{1,0,2:T(8,128)S(1)} copy-done((f32[512,256,16]{1,0,2:T(8,128)S(1)}, f32[512,256,16]{1,0,2:T(8,128)}, u32[]{:S(2)}) %copy-start) | copy-done | bytes 8388632 | tf_op jit(solution)/shard_map/while
  50.8 5.1 %bitcast_add_fusion.6 = f32[1,16,256,128]{3,2,1,0:T(8,128)} fusion(f32[1,16,256,128]{3,2,1,0:T(8,128)} %get-tuple-element.235, f32[512,256,16]{1,0,2:T(8,128)S(1)} %copy-done, f32[16,256]{1,0:T(8,128)S(1)} %bitcast.115, pred[256,512]{0,1:T(8,128)(4,1)S(1)} %broadcast_compare_fusion.2, f32[16,256]{1,0:T(8,128)S(1)} %get-tuple-element.220, ...), kind=kOutput, calls=%fused_computation.9.clone.1 | convolution fusion | flops 548929536 | bytes 12877829 | tf_op jit(solution)/shard_map/while/body/eval_jaxpr/hgqk,khd->hgqd/dot_general | solution.py:85
  56.1 4.6 %fusion.36 = (f32[16,256]{1,0:T(8,128)S(1)}, f32[512,256,16]{1,0,2:T(8,128)}) fusion(pred[256,512]{0,1:T(8,128)(4,1)S(1)} %broadcast_compare_fusion.2, bf16[256,1,16,128]{3,0,2,1:T(8,128)(2,1)S(1)} %get-tuple-element.249, bf16[4,512,1,128]{3,1,2,0:T(8,128)(2,1)S(1)} %get-tuple-element.248, s32[]{:T(128)S(6)} %copy.48), kind=kOutput, calls=%fused_computation.3.clone.1 | convolution fusion | flops 543158272 | bytes 9715716 | tf_op jit(solution)/shard_map/while/body/eval_jaxpr/qhgd,khd->hgqk/dot_general | solution.py:76
  60.7 4.6 %fusion.38 = f32[16,256]{1,0:T(8,128)S(1)} fusion(f32[512,256,16]{1,0,2:T(8,128)} %get-tuple-element.219, f32[16,256]{1,0:T(8,128)S(1)} %bitcast.114, pred[256,512]{0,1:T(8,128)(4,1)S(1)} %broadcast_compare_fusion.2), kind=kLoop, calls=%fused_computation.5.clone.1 | loop fusion | flops 10481664 | bytes 8552448 | tf_op jit(solution)/shard_map/while/body/eval_jaxpr/reduce_sum | solution.py:84
  65.3 1.2 %copy-done = f32[512,256,16]{1,0,2:T(8,128)S(1)} copy-done((f32[512,256,16]{1,0,2:T(8,128)S(1)}, f32[512,256,16]{1,0,2:T(8,128)}, u32[]{:S(2)}) %copy-start) | copy-done | bytes 8388632 | tf_op jit(solution)/shard_map/while
  66.5 5.1 %bitcast_add_fusion.6 = f32[1,16,256,128]{3,2,1,0:T(8,128)} fusion(f32[1,16,256,128]{3,2,1,0:T(8,128)} %get-tuple-element.235, f32[512,256,16]{1,0,2:T(8,128)S(1)} %copy-done, f32[16,256]{1,0:T(8,128)S(1)} %bitcast.115, pred[256,512]{0,1:T(8,128)(4,1)S(1)} %broadcast_compare_fusion.2, f32[16,256]{1,0:T(8,128)S(1)} %get-tuple-element.220, ...), kind=kOutput, calls=%fused_computation.9.clone.1 | convolution fusion | flops 548929536 | bytes 12877829 | tf_op jit(solution)/shard_map/while/body/eval_jaxpr/hgqk,khd->hgqd/dot_general | solution.py:85
  71.8 4.6 %fusion.36 = (f32[16,256]{1,0:T(8,128)S(1)}, f32[512,256,16]{1,0,2:T(8,128)}) fusion(pred[256,512]{0,1:T(8,128)(4,1)S(1)} %broadcast_compare_fusion.2, bf16[256,1,16,128]{3,0,2,1:T(8,128)(2,1)S(1)} %get-tuple-element.249, bf16[4,512,1,128]{3,1,2,0:T(8,128)(2,1)S(1)} %get-tuple-element.248, s32[]{:T(128)S(6)} %copy.48), kind=kOutput, calls=%fused_computation.3.clone.1 | convolution fusion | flops 543158272 | bytes 9715716 | tf_op jit(solution)/shard_map/while/body/eval_jaxpr/qhgd,khd->hgqk/dot_general | solution.py:76
  76.4 4.6 %fusion.38 = f32[16,256]{1,0:T(8,128)S(1)} fusion(f32[512,256,16]{1,0,2:T(8,128)} %get-tuple-element.219, f32[16,256]{1,0:T(8,128)S(1)} %bitcast.114, pred[256,512]{0,1:T(8,128)(4,1)S(1)} %broadcast_compare_fusion.2), kind=kLoop, calls=%fused_computation.5.clone.1 | loop fusion | flops 10481664 | bytes 8552448 | tf_op jit(solution)/shard_map/while/body/eval_jaxpr/reduce_sum | solution.py:84
  81.0 1.2 %copy-done = f32[512,256,16]{1,0,2:T(8,128)S(1)} copy-done((f32[512,256,16]{1,0,2:T(8,128)S(1)}, f32[512,256,16]{1,0,2:T(8,128)}, u32[]{:S(2)}) %copy-start) | copy-done | bytes 8388632 | tf_op jit(solution)/shard_map/while
  82.2 5.1 %bitcast_add_fusion.6 = f32[1,16,256,128]{3,2,1,0:T(8,128)} fusion(f32[1,16,256,128]{3,2,1,0:T(8,128)} %get-tuple-element.235, f32[512,256,16]{1,0,2:T(8,128)S(1)} %copy-done, f32[16,256]{1,0:T(8,128)S(1)} %bitcast.115, pred[256,512]{0,1:T(8,128)(4,1)S(1)} %broadcast_compare_fusion.2, f32[16,256]{1,0:T(8,128)S(1)} %get-tuple-element.220, ...), kind=kOutput, calls=%fused_computation.9.clone.1 | convolution fusion | flops 548929536 | bytes 12877829 | tf_op jit(solution)/shard_map/while/body/eval_jaxpr/hgqk,khd->hgqd/dot_general | solution.py:85
  87.3 1.9 %fusion.25 = bf16[256,1,16,128]{3,0,2,1:T(8,128)(2,1)S(1)} fusion(f32[1,16,256,128]{3,2,1,0:T(8,128)} %get-tuple-element.51, f32[16,256]{1,0:T(8,128)S(1)} %bitcast.123), kind=kLoop, calls=%fused_computation.36 | loop fusion | flops 1048576 | bytes 3162112 | tf_op jit(solution)/shard_map/convert_element_type | solution.py:107
  89.3 0.7 copy.35
  90.0 1.2 %copy.43 = bf16[32,8,16,128]{3,1,2,0:T(8,128)(2,1)} copy(bf16[32,8,16,128]{3,2,1,0:T(8,128)(2,1)S(1)} %bitcast.116) | data formatting | bytes 2097152
  91.2 0.6 fusion.27
  93.3 14.8 %all_gather.11 = bf16[2,4,2,128,128]{4,3,2,1,0:T(8,128)(2,1)S(1)} all-gather(bf16[2,1,2,128,128]{4,3,2,1,0:T(8,128)(2,1)S(1)} %pad_maximum_fusion), channel_id=1, replica_groups=mesh['ctx'=8,'page'=4] {'page'}, dimensions={1}, use_global_device_ids=true | all-gather | bytes 655360 | tf_op jit(solution)/shard_map/all_gather | solution.py:104
  108.1 0.2 fusion.23
  108.3 1.0 fusion.24
  109.3 0.7 copy.37
  (44 shorter events, 1.1 us)
Async XLA Ops:
  25.6 65.6 %copy-start.1 = (s32[16]{0:T(128)S(1)}, s32[16]{0:T(128)}, u32[]{:S(2)}) copy-start(s32[16]{0:T(128)} %param.11) | copy-start | bytes 196
  30.5 5.8 %copy-start = (f32[512,256,16]{1,0,2:T(8,128)S(1)}, f32[512,256,16]{1,0,2:T(8,128)}, u32[]{:S(2)}) copy-start(f32[512,256,16]{1,0,2:T(8,128)} %get-tuple-element.219) | copy-start | bytes 25165828 | tf_op jit(solution)/shard_map/while
  45.0 5.8 %copy-start = (f32[512,256,16]{1,0,2:T(8,128)S(1)}, f32[512,256,16]{1,0,2:T(8,128)}, u32[]{:S(2)}) copy-start(f32[512,256,16]{1,0,2:T(8,128)} %get-tuple-element.219) | copy-start | bytes 25165828 | tf_op jit(solution)/shard_map/while
  60.7 5.8 %copy-start = (f32[512,256,16]{1,0,2:T(8,128)S(1)}, f32[512,256,16]{1,0,2:T(8,128)}, u32[]{:S(2)}) copy-start(f32[512,256,16]{1,0,2:T(8,128)} %get-tuple-element.219) | copy-start | bytes 25165828 | tf_op jit(solution)/shard_map/while
  76.4 5.8 %copy-start = (f32[512,256,16]{1,0,2:T(8,128)S(1)}, f32[512,256,16]{1,0,2:T(8,128)}, u32[]{:S(2)}) copy-start(f32[512,256,16]{1,0,2:T(8,128)} %get-tuple-element.219) | copy-start | bytes 25165828 | tf_op jit(solution)/shard_map/while
where the time goes:
time: 112 us; the launch traced here: 110 us
  matrix products  37.4 us (33%)
  blocking collectives  35.9 us (32%)
  other arithmetic  24.9 us (22%)
  local copies, waits for them, and re-layouts  9.68 us (9%)
  between operations  2.05 us (2%)
    dot_general x4, matrix products, step(): jnp.einsum('hgqk,khd->hgqd', weight.astype(jnp.bfloat16), value_block, pr...  19.1 us
    reduce_sum x4, other arithmetic, step(): total = total * factor + jnp.sum(weight, axis=-1)  18.4 us
    dot_general x4, matrix products, step(): jnp.einsum('qhgd,khd->hgqk', query_heads, key_block, preferred_element_ty...  18.3 us
    all_gather x1, blocking collectives, on_device(): raw = lax.all_gather(local_raw, 'page', axis=1, tiled=True)  14.8 us
    all_gather x1, blocking collectives, on_device(): key_piece = lax.all_gather(keys, 'ctx', axis=0, tiled=True)  11.5 us
    all_gather x1, blocking collectives, on_device(): value_piece = lax.all_gather(values, 'ctx', axis=0, tiled=True)  9.53 us
    while x12, local copies, waits for them, and re-layouts  4.76 us
    unnamed x7, local copies, waits for them, and re-layouts  4.13 us

commit v1 on v0

v1 whole, which is shorter than its diff:
```python
import functools
import math

import jax
import jax.numpy as jnp
from jax import lax
from jax.experimental import pallas as pl
from jax.experimental.pallas import tpu as pltpu
from jax.sharding import PartitionSpec as P

DH = 128
PAGE = 128
SPAN = 128
HIDE = -1e30
MESH = pl.DeviceIdType.MESH


def kernel(
    n, n_page, heads, table_ref, slots_ref, q_ref, k_ref, v_ref,
    out_ref, cache_ref, scales_ref,
    kbuf, vbuf, kmask, vone, acc, top, send, recv, own_sem, page_send, page_recv,
):
    chips = n // 2
    spans = k_ref.shape[0]
    wide = 2 * spans * SPAN
    per = math.gcd(heads, 4)
    groups = heads // per
    size = per * SPAN
    me = lax.axis_index("ctx")
    page = lax.axis_index("page")
    chip = me // 2
    core = me % 2
    sibling = 2 * chip + 1 - core
    rate = DH ** (-0.5) * math.log2(math.e)

    def ahead(d):
        return 2 * ((chip + d) % chips) + core

    def behind(d, c):
        return 2 * ((chip + chips - d) % chips) + c

    barrier = pltpu.get_barrier_semaphore()
    for d in range(1, chips):
        pl.semaphore_signal(barrier, inc=1, device_id={"ctx": ahead(d)}, device_id_type=MESH)
    pl.semaphore_signal(barrier, inc=1, device_id={"ctx": sibling}, device_id_type=MESH)
    for d in range(1, n_page):
        pl.semaphore_signal(
            barrier, inc=1, device_id={"page": (page + d) % n_page}, device_id_type=MESH
        )
    pl.semaphore_wait(barrier, chips + n_page - 1)

    def slot(buf, owner):
        return buf.at[pl.ds(owner * spans, spans)]

    def remote(src, buf, owner, index, j, target):
        return pltpu.make_async_remote_copy(
            src_ref=src,
            dst_ref=slot(buf, owner),
            send_sem=send.at[index, j],
            recv_sem=recv.at[index, j],
            device_id={"ctx": target},
            device_id_type=MESH,
        )

    pairs = ((k_ref, kbuf), (v_ref, vbuf))
    started = []
    local = []
    for d in range(1, chips):
        for j, (src, buf) in enumerate(pairs):
            copy = remote(src, buf, me, d, j, ahead(d))
            copy.start()
            started.append(copy)
    for j, (src, buf) in enumerate(pairs):
        copy = remote(src, buf, me, 0, j, sibling)
        copy.start()
        started.append(copy)
        copy = pltpu.make_async_copy(src, slot(buf, me), own_sem.at[j])
        copy.start()
        local.append(copy)

    rows_at = lax.broadcasted_iota(jnp.int32, (SPAN, SPAN), 0)
    cols_at = lax.broadcasted_iota(jnp.int32, (SPAN, SPAN), 1)
    eye = jnp.where(rows_at == cols_at, 1.0, 0.0).astype(jnp.bfloat16)
    vone[:, DH:] = jnp.ones((wide, DH), jnp.bfloat16)

    def chunk(d, first):
        owner = (chip + chips - d) % chips
        begin = owner * 2 * spans
        for t in range(2 * spans):
            place = pl.ds(t * SPAN, SPAN)
            piece = kbuf[begin + t]
            vone[place, :DH] = vbuf[begin + t]
            for i in range(spans):
                gap = (table_ref[me * spans + i] - table_ref[begin + t]) * SPAN
                kmask[i, place, :DH] = piece
                kmask[i, place, DH:] = jnp.where(rows_at - cols_at > gap, HIDE, 0.0).astype(
                    jnp.bfloat16
                )

        @pl.loop(0, groups)
        def _(g):
            for i in range(spans):
                lines = pl.ds(i * SPAN, SPAN)
                query = jnp.concatenate(
                    [
                        jnp.concatenate(
                            [
                                q_ref[lines, pl.ds(pl.multiple_of((g * per + h) * DH, DH), DH)],
                                eye,
                            ],
                            axis=1,
                        )
                        for h in range(per)
                    ],
                    axis=0,
                )
                score = lax.dot_general(
                    query, kmask[i], (((1,), (1,)), ((), ())), preferred_element_type=jnp.float32
                )
                high = jnp.broadcast_to(jnp.max(score, axis=1, keepdims=True), (size, DH))
                if not first:
                    old = top[g, i]
                    high = jnp.maximum(high, old)
                weight = jnp.concatenate(
                    [
                        jnp.exp2((score[:, t * SPAN : (t + 1) * SPAN] - high) * rate).astype(
                            jnp.bfloat16
                        )
                        for t in range(2 * spans)
                    ],
                    axis=1,
                )
                update = jnp.dot(weight, vone[...], preferred_element_type=jnp.float32)
                top[g, i] = high
                if first:
                    acc[g, i] = update
                else:
                    factor = jnp.exp2((old - high) * rate)
                    acc[g, i, :, :DH] = acc[g, i, :, :DH] * factor + update[:, :DH]
                    acc[g, i, :, DH:] = acc[g, i, :, DH:] * factor + update[:, DH:]

    for copy in local:
        copy.wait()
    for j, (src, buf) in enumerate(pairs):
        remote(src, buf, sibling, 0, j, sibling).wait_recv()
    chunk(0, True)

    for d in range(1, chips):
        for j, (src, buf) in enumerate(pairs):
            origin = behind(d, core)
            remote(src, buf, origin, d, j, sibling).wait_recv()
            copy = remote(slot(buf, origin), buf, origin, chips - 1 + d, j, sibling)
            copy.start()
            started.append(copy)
    for d in range(1, chips):
        for j, (src, buf) in enumerate(pairs):
            remote(src, buf, behind(d, 1 - core), chips - 1 + d, j, sibling).wait_recv()

    for s in range(spans):
        wanted = jnp.int32(0)
        for p in range(slots_ref.shape[0]):
            wanted = jnp.where(slots_ref[p] == me * spans + s, p, wanted)
        for j, buf in enumerate((kbuf, vbuf)):
            raw = buf[wanted].astype(jnp.float32)
            level = jnp.max(jnp.max(jnp.abs(raw), axis=0, keepdims=True), axis=1, keepdims=True)
            level = level + 1e-06
            cache_ref[page, s, j] = (raw / level).astype(jnp.bfloat16)
            scales_ref[page, s, j] = jnp.broadcast_to(level, (8, DH))

    def pages(index, target):
        return [
            pltpu.make_async_remote_copy(
                src_ref=ref.at[page],
                dst_ref=ref.at[page],
                send_sem=page_send.at[index, j],
                recv_sem=page_recv.at[index, j],
                device_id={"page": target},
                device_id_type=MESH,
            )
            for j, ref in enumerate((cache_ref, scales_ref))
        ]

    def arrived(index):
        origin = (page + n_page - index) % n_page
        for j, ref in enumerate((cache_ref, scales_ref)):
            pltpu.make_async_remote_copy(
                src_ref=ref.at[origin],
                dst_ref=ref.at[origin],
                send_sem=page_send.at[index, j],
                recv_sem=page_recv.at[index, j],
                device_id={"page": (page + index) % n_page},
                device_id_type=MESH,
            ).wait_recv()

    for d in range(1, chips):
        chunk(d, False)
        if d == 1:
            for index in range(1, n_page):
                for copy in pages(index, (page + index) % n_page):
                    copy.start()
                    started.append(copy)

    @pl.loop(0, groups)
    def _(g):
        for i in range(spans):
            for h in range(per):
                lines = pl.ds(h * SPAN, SPAN)
                out_ref[
                    pl.ds(i * SPAN, SPAN), pl.ds(pl.multiple_of((g * per + h) * DH, DH), DH)
                ] = (acc[g, i, lines, :DH] / acc[g, i, lines, DH:]).astype(jnp.bfloat16)

    for index in range(1, n_page):
        arrived(index)
    for copy in started:
        copy.wait_send()


def on_device(n, n_page, queries, keys, values, span_table, page_slots):
    rows = queries.shape[0]
    heads = queries.shape[1] // DH
    spans = rows // SPAN
    per = math.gcd(heads, 4)
    groups = heads // per
    chips = n // 2
    wide = 2 * rows
    vmem = pl.BlockSpec(memory_space=pltpu.VMEM)
    smem = pl.BlockSpec(memory_space=pltpu.SMEM)
    attended, cache, scales = pl.pallas_call(
        functools.partial(kernel, n, n_page, heads),
        out_shape=(
            jax.ShapeDtypeStruct((rows, heads * DH), jnp.bfloat16),
            jax.ShapeDtypeStruct((n_page, spans, 2, PAGE, DH), jnp.bfloat16),
            jax.ShapeDtypeStruct((n_page, spans, 2, 8, DH), jnp.float32),
        ),
        in_specs=[smem, smem, vmem, vmem, vmem],
        out_specs=(vmem, vmem, vmem),
        scratch_shapes=[
            pltpu.VMEM((n * spans, SPAN, DH), jnp.bfloat16),
            pltpu.VMEM((n * spans, SPAN, DH), jnp.bfloat16),
            pltpu.VMEM((spans, wide, 2 * DH), jnp.bfloat16),
            pltpu.VMEM((wide, 2 * DH), jnp.bfloat16),
            pltpu.VMEM((groups, spans, per * SPAN, 2 * DH), jnp.float32),
            pltpu.VMEM((groups, spans, per * SPAN, DH), jnp.float32),
            pltpu.SemaphoreType.DMA((n, 2)),
            pltpu.SemaphoreType.DMA((n, 2)),
            pltpu.SemaphoreType.DMA((2,)),
            pltpu.SemaphoreType.DMA((n_page, 2)),
            pltpu.SemaphoreType.DMA((n_page, 2)),
        ],
        compiler_params=pltpu.CompilerParams(
            collective_id=0, has_side_effects=True, vmem_limit_bytes=48 * 1024 * 1024
        ),
    )(
        span_table,
        page_slots,
        queries,
        keys.reshape(spans, SPAN, DH),
        values.reshape(spans, SPAN, DH),
    )
    cache = cache.transpose(1, 0, 2, 3, 4)
    scales = scales[:, :, :, 0, 0].transpose(1, 0, 2)
    return attended, cache, scales


def solution(mesh):
    placed = (P("ctx", "page"), P("ctx", "page"), P("ctx", "page"), P(), P())
    return jax.shard_map(
        functools.partial(on_device, mesh.shape["ctx"], mesh.shape["page"]),
        mesh=mesh,
        in_specs=placed,
        out_specs=(P("ctx", "page"), P("ctx", None, None, None, None), P("ctx", None, None)),
        check_vma=False,
    )
```

time: 112 us -> 38.4 us (0.34)
  the two profiles are of different devices: /device:TPU:1 before, /device:TPU:13 now
where the time goes in v1:
time: 38.4 us; the launch traced here: 38.1 us
  Pallas kernels  31.4 us (82%)
  local copies, waits for them, and re-layouts  6.05 us (16%)
  between operations  0.66 us (2%)
    pallas_call x1, Pallas kernels, on_device(): pl.pallas_call(functools.partial(kernel, n, n_page, heads), out_shape=(ja...  31.4 us
    unnamed x12, local copies, waits for them, and re-layouts  5.36 us

profile of v1, /device:TPU:13, one launch (start us, length us, event | category | flops | bytes accessed | tf_op | source)
XLA Modules:
  0.0 38.1 jit_solution(5903375200833898809)
XLA Ops:
  0.6 0.0 copy-start.3
  0.6 0.0 copy-start.4
  0.7 0.6 %copy-done.3 = s32[16]{0:T(128)S(1)} copy-done((s32[16]{0:T(128)S(1)}, s32[16]{0:T(128)}, u32[]{:S(2)}) %copy-start.3) | copy-done | bytes 88
  1.3 0.0 copy-done.4
  1.3 0.0 copy-start
  1.3 1.2 %copy-done = bf16[256,2048]{1,0:T(8,128)(2,1)S(1)} copy-done((bf16[256,2048]{1,0:T(8,128)(2,1)S(1)}, bf16[256,2048]{1,0:T(8,128)(2,1)}, u32[]{:S(2)}) %copy-start) | copy-done | bytes 1048600
  2.5 0.0 copy-start.1
  2.5 0.8 %copy-done.1 = bf16[256,128]{1,0:T(8,128)(2,1)S(1)} copy-done((bf16[256,128]{1,0:T(8,128)(2,1)S(1)}, bf16[256,128]{1,0:T(8,128)(2,1)}, u32[]{:S(2)}) %copy-start.1) | copy-done | bytes 65560
  3.4 0.0 copy-start.2
  3.4 0.8 %copy-done.2 = bf16[256,128]{1,0:T(8,128)(2,1)S(1)} copy-done((bf16[256,128]{1,0:T(8,128)(2,1)S(1)}, bf16[256,128]{1,0:T(8,128)(2,1)}, u32[]{:S(2)}) %copy-start.2) | copy-done | bytes 65560
  4.2 31.4 %shard_map.76 = (bf16[256,2048]{1,0:T(8,128)(2,1)S(1)}, bf16[4,2,2,128,128]{4,3,2,1,0:T(8,128)(2,1)S(1)}, f32[4,2,2,8,128]{4,3,2,1,0:T(8,128)S(1)}) custom-call(s32[16]{0:T(128)S(1)} %copy-done.3, s32[16]{0:T(128)S(1)} %copy-done.4, bf16[256,2048]{1,0:T(8,128)(2,1)S(1)} %copy-done, bf16[2,128,128]{2,1,0:T(8,128)(2,1)S(1)} %bitcast.7, ...), custom_call_target="tpu_custom_call" | custom-call | tf_op jit(solution)/shard_map/pallas_call | solution.py:228
  35.7 0.8 %copy.9 = bf16[2,4,2,128,128]{4,3,2,1,0:T(8,128)(2,1)} copy(bf16[2,4,2,128,128]{4,3,2,0,1:T(8,128)(2,1)S(1)} %bitcast.6) | data formatting | bytes 1048576
  36.5 0.7 %copy.8 = f32[4,2,2,1,1]{0,2,4,3,1:T(2,128)} copy(f32[4,2,2,1,1]{4,3,2,1,0:T(1,128)S(1)} %slice.3) | data formatting | bytes 128 | tf_op jit(solution)/shard_map/slice | solution.py:261
  37.2 1.0 %copy.11 = bf16[256,2048]{1,0:T(8,128)(2,1)} copy(bf16[256,2048]{1,0:T(8,128)(2,1)S(1)} %get-tuple-element.15) | data formatting | bytes 2097152
  (1 shorter events, 0.0 us)
Async XLA Ops:
  0.6 0.7 %copy-start.3 = (s32[16]{0:T(128)S(1)}, s32[16]{0:T(128)}, u32[]{:S(2)}) copy-start(s32[16]{0:T(128)} %table_ref.1) | copy-start | bytes 196
  0.6 0.7 %copy-start.4 = (s32[16]{0:T(128)S(1)}, s32[16]{0:T(128)}, u32[]{:S(2)}) copy-start(s32[16]{0:T(128)} %slots_ref.1) | copy-start | bytes 196
  1.3 1.2 %copy-start = (bf16[256,2048]{1,0:T(8,128)(2,1)S(1)}, bf16[256,2048]{1,0:T(8,128)(2,1)}, u32[]{:S(2)}) copy-start(bf16[256,2048]{1,0:T(8,128)(2,1)} %q_ref.1) | copy-start | bytes 3145732
  2.5 0.8 %copy-start.1 = (bf16[256,128]{1,0:T(8,128)(2,1)S(1)}, bf16[256,128]{1,0:T(8,128)(2,1)}, u32[]{:S(2)}) copy-start(bf16[256,128]{1,0:T(8,128)(2,1)} %param.6) | copy-start | bytes 196612
  3.4 0.8 %copy-start.2 = (bf16[256,128]{1,0:T(8,128)(2,1)S(1)}, bf16[256,128]{1,0:T(8,128)(2,1)}, u32[]{:S(2)}) copy-start(bf16[256,128]{1,0:T(8,128)(2,1)} %param.7) | copy-start | bytes 196612

commit v2 on v1

--- a/solution.py
+++ b/solution.py
@@ -16,8 +16,9 @@
 
 
 def kernel(
-    n, n_page, heads, table_ref, slots_ref, q_ref, k_ref, v_ref,
+    n, n_page, heads, table_in, slots_in, q_in, k_ref, v_ref,
     out_ref, cache_ref, scales_ref,
+    table_ref, slots_ref, q_ref,
     kbuf, vbuf, kmask, vone, acc, top, send, recv, own_sem, page_send, page_recv,
 ):
     chips = n // 2
@@ -39,6 +40,13 @@
     def behind(d, c):
         return 2 * ((chip + chips - d) % chips) + c
 
+    local = []
+
+    def fetch(src, dst, j):
+        copy = pltpu.make_async_copy(src, dst, own_sem.at[j])
+        copy.start()
+        local.append(copy)
+
     barrier = pltpu.get_barrier_semaphore()
     for d in range(1, chips):
         pl.semaphore_signal(barrier, inc=1, device_id={"ctx": ahead(d)}, device_id_type=MESH)
@@ -47,10 +55,16 @@
         pl.semaphore_signal(
             barrier, inc=1, device_id={"page": (page + d) % n_page}, device_id_type=MESH
         )
-    pl.semaphore_wait(barrier, chips + n_page - 1)
 
     def slot(buf, owner):
         return buf.at[pl.ds(owner * spans, spans)]
+
+    fetch(k_ref, slot(kbuf, me), 0)
+    fetch(v_ref, slot(vbuf, me), 1)
+    fetch(table_in, table_ref, 2)
+    fetch(slots_in, slots_ref, 3)
+    fetch(q_in, q_ref, 4)
+    pl.semaphore_wait(barrier, chips + n_page - 1)
 
     def remote(src, buf, owner, index, j, target):
         return pltpu.make_async_remote_copy(
@@ -64,7 +78,6 @@
 
     pairs = ((k_ref, kbuf), (v_ref, vbuf))
     started = []
-    local = []
     for d in range(1, chips):
         for j, (src, buf) in enumerate(pairs):
             copy = remote(src, buf, me, d, j, ahead(d))
@@ -74,9 +87,6 @@
         copy = remote(src, buf, me, 0, j, sibling)
         copy.start()
         started.append(copy)
-        copy = pltpu.make_async_copy(src, slot(buf, me), own_sem.at[j])
-        copy.start()
-        local.append(copy)
 
     rows_at = lax.broadcasted_iota(jnp.int32, (SPAN, SPAN), 0)
     cols_at = lax.broadcasted_iota(jnp.int32, (SPAN, SPAN), 1)
@@ -97,8 +107,7 @@
                     jnp.bfloat16
                 )
 
-        @pl.loop(0, groups)
-        def _(g):
+        def attend_group(g):
             for i in range(spans):
                 lines = pl.ds(i * SPAN, SPAN)
                 query = jnp.concatenate(
@@ -139,11 +148,13 @@
                     acc[g, i, :, :DH] = acc[g, i, :, :DH] * factor + update[:, :DH]
                     acc[g, i, :, DH:] = acc[g, i, :, DH:] * factor + update[:, DH:]
 
+        return lambda: pl.loop(0, groups)(attend_group)
+
     for copy in local:
         copy.wait()
     for j, (src, buf) in enumerate(pairs):
         remote(src, buf, sibling, 0, j, sibling).wait_recv()
-    chunk(0, True)
+    chunk(0, True)()
 
     for d in range(1, chips):
         for j, (src, buf) in enumerate(pairs):
@@ -193,12 +204,13 @@
             ).wait_recv()
 
     for d in range(1, chips):
-        chunk(d, False)
+        attend = chunk(d, False)
         if d == 1:
             for index in range(1, n_page):
                 for copy in pages(index, (page + index) % n_page):
                     copy.start()
                     started.append(copy)
+        attend()
 
     @pl.loop(0, groups)
     def _(g):
@@ -224,7 +236,7 @@
     chips = n // 2
     wide = 2 * rows
     vmem = pl.BlockSpec(memory_space=pltpu.VMEM)
-    smem = pl.BlockSpec(memory_space=pltpu.SMEM)
+    hbm = pl.BlockSpec(memory_space=pltpu.HBM)
     attended, cache, scales = pl.pallas_call(
         functools.partial(kernel, n, n_page, heads),
         out_shape=(
@@ -232,9 +244,12 @@
             jax.ShapeDtypeStruct((n_page, spans, 2, PAGE, DH), jnp.bfloat16),
             jax.ShapeDtypeStruct((n_page, spans, 2, 8, DH), jnp.float32),
         ),
-        in_specs=[smem, smem, vmem, vmem, vmem],
+        in_specs=[hbm] * 5,
         out_specs=(vmem, vmem, vmem),
         scratch_shapes=[
+            pltpu.SMEM(span_table.shape, jnp.int32),
+            pltpu.SMEM(page_slots.shape, jnp.int32),
+            pltpu.VMEM(queries.shape, jnp.bfloat16),
             pltpu.VMEM((n * spans, SPAN, DH), jnp.bfloat16),
             pltpu.VMEM((n * spans, SPAN, DH), jnp.bfloat16),
             pltpu.VMEM((spans, wide, 2 * DH), jnp.bfloat16),
@@ -243,12 +258,12 @@
             pltpu.VMEM((groups, spans, per * SPAN, DH), jnp.float32),
             pltpu.SemaphoreType.DMA((n, 2)),
             pltpu.SemaphoreType.DMA((n, 2)),
-            pltpu.SemaphoreType.DMA((2,)),
+            pltpu.SemaphoreType.DMA((5,)),
             pltpu.SemaphoreType.DMA((n_page, 2)),
             pltpu.SemaphoreType.DMA((n_page, 2)),
         ],
         compiler_params=pltpu.CompilerParams(
-            collective_id=0, has_side_effects=True, vmem_limit_bytes=48 * 1024 * 1024
+            collective_id=0, has_side_effects=True, vmem_limit_bytes=67043328
         ),
     )(
         span_table,

time: 38.4 us -> 34.7 us (0.904)
  the two profiles are of different devices: /device:TPU:13 before, /device:TPU:1 now
where the time goes in v2:
time: 34.7 us; the launch traced here: 34.5 us
  Pallas kernels  29.4 us (85%)
  local copies, waits for them, and re-layouts  4.47 us (13%)
  between operations  0.65 us (2%)
    pallas_call x1, Pallas kernels, on_device(): pl.pallas_call(functools.partial(kernel, n, n_page, heads), out_shape=(ja...  29.4 us
    unnamed x4, local copies, waits for them, and re-layouts  2.95 us
    slice x2, local copies, waits for them, and re-layouts, on_device(): scales = scales[:, :, :, 0, 0].transpose(1, 0, 2)  1.53 us

profile of v2, /device:TPU:1, one launch (start us, length us, event | category | flops | bytes accessed | tf_op | source)
XLA Modules:
  0.0 34.5 jit_solution(4315890753491343187)
XLA Ops:
  0.6 29.4 %shard_map.76 = (bf16[256,2048]{1,0:T(8,128)(2,1)}, bf16[4,2,2,128,128]{4,3,2,1,0:T(8,128)(2,1)}, f32[4,2,2,8,128]{4,3,2,1,0:T(8,128)}) custom-call(s32[16]{0:T(128)} %table_in.1, s32[16]{0:T(128)} %slots_in.1, bf16[256,2048]{1,0:T(8,128)(2,1)} %q_in.1, bf16[2,128,128]{2,1,0:T(8,128)(2,1)} %bitcast.7, bf16[2,128,128]{2,1,0:T(8,128)(2,1)} %bitcast.8), custom_call_target="tpu_custom_call" | custom-call | tf_op jit(solution)/shard_map/pallas_call | solution.py:240
  30.1 0.0 copy-start
  30.1 2.0 %copy.9 = bf16[2,4,2,128,128]{4,3,2,1,0:T(8,128)(2,1)} copy(bf16[2,4,2,128,128]{4,3,2,0,1:T(8,128)(2,1)} %bitcast.6) | data formatting | bytes 1048576
  32.0 0.8 %slice.3 = f32[4,2,2,1,1]{4,3,2,1,0:T(1,128)S(1)} slice(f32[4,2,2,8,128]{4,3,2,1,0:T(8,128)} %get-tuple-element.8), slice={[0:4], [0:2], [0:2], [0:1], [0:1]} | slice | bytes 128 | tf_op jit(solution)/shard_map/slice | solution.py:276
  32.9 0.7 %copy.8 = f32[4,2,2,1,1]{0,2,4,3,1:T(2,128)} copy(f32[4,2,2,1,1]{4,3,2,1,0:T(1,128)S(1)} %slice.3) | data formatting | bytes 128 | tf_op jit(solution)/shard_map/slice | solution.py:276
  33.6 0.0 copy-done
  33.6 1.0 %copy.11 = bf16[256,2048]{1,0:T(8,128)(2,1)} copy(bf16[256,2048]{1,0:T(8,128)(2,1)S(1)} %copy-done) | data formatting | bytes 2097152
Async XLA Ops:
  30.1 3.5 %copy-start = (bf16[256,2048]{1,0:T(8,128)(2,1)S(1)}, bf16[256,2048]{1,0:T(8,128)(2,1)}, u32[]{:S(2)}) copy-start(bf16[256,2048]{1,0:T(8,128)(2,1)} %get-tuple-element.15) | copy-start | bytes 3145732

commit v3 on v2

--- a/solution.py
+++ b/solution.py
@@ -20,6 +20,7 @@
     out_ref, cache_ref, scales_ref,
     table_ref, slots_ref, q_ref,
     kbuf, vbuf, kmask, vone, acc, top, send, recv, own_sem, page_send, page_recv,
+    level_send, level_recv,
 ):
     chips = n // 2
     spans = k_ref.shape[0]
@@ -34,11 +35,15 @@
     sibling = 2 * chip + 1 - core
     rate = DH ** (-0.5) * math.log2(math.e)
 
-    def ahead(d):
-        return 2 * ((chip + d) % chips) + core
-
-    def behind(d, c):
-        return 2 * ((chip + chips - d) % chips) + c
+    def partner(d):
+        other, bit = 0, 1
+        while bit < chips:
+            other = other + (chip // bit + d // bit) % 2 * bit
+            bit *= 2
+        return other
+
+    def peer(d, c):
+        return 2 * partner(d) + c
 
     local = []
 
@@ -49,7 +54,7 @@
 
     barrier = pltpu.get_barrier_semaphore()
     for d in range(1, chips):
-        pl.semaphore_signal(barrier, inc=1, device_id={"ctx": ahead(d)}, device_id_type=MESH)
+        pl.semaphore_signal(barrier, inc=1, device_id={"ctx": peer(d, core)}, device_id_type=MESH)
     pl.semaphore_signal(barrier, inc=1, device_id={"ctx": sibling}, device_id_type=MESH)
     for d in range(1, n_page):
         pl.semaphore_signal(
@@ -80,7 +85,7 @@
     started = []
     for d in range(1, chips):
         for j, (src, buf) in enumerate(pairs):
-            copy = remote(src, buf, me, d, j, ahead(d))
+            copy = remote(src, buf, me, d, j, peer(d, core))
             copy.start()
             started.append(copy)
     for j, (src, buf) in enumerate(pairs):
@@ -94,7 +99,7 @@
     vone[:, DH:] = jnp.ones((wide, DH), jnp.bfloat16)
 
     def chunk(d, first):
-        owner = (chip + chips - d) % chips
+        owner = partner(d)
         begin = owner * 2 * spans
         for t in range(2 * spans):
             place = pl.ds(t * SPAN, SPAN)
@@ -156,16 +161,28 @@
         remote(src, buf, sibling, 0, j, sibling).wait_recv()
     chunk(0, True)()
 
-    for d in range(1, chips):
+    def relay(d):
         for j, (src, buf) in enumerate(pairs):
-            origin = behind(d, core)
+            origin = peer(d, core)
             remote(src, buf, origin, d, j, sibling).wait_recv()
             copy = remote(slot(buf, origin), buf, origin, chips - 1 + d, j, sibling)
             copy.start()
             started.append(copy)
-    for d in range(1, chips):
+
+    def landed(d):
         for j, (src, buf) in enumerate(pairs):
-            remote(src, buf, behind(d, 1 - core), chips - 1 + d, j, sibling).wait_recv()
+            remote(src, buf, peer(d, 1 - core), chips - 1 + d, j, sibling).wait_recv()
+
+    half = chips // 2
+    for d in range(1, half + 1):
+        relay(d)
+    for d in range(1, half):
+        landed(d)
+        chunk(d, False)()
+    for d in range(half + 1, chips):
+        relay(d)
+    for d in range(half, chips):
+        landed(d)
 
     for s in range(spans):
         wanted = jnp.int32(0)
@@ -175,42 +192,67 @@
             raw = buf[wanted].astype(jnp.float32)
             level = jnp.max(jnp.max(jnp.abs(raw), axis=0, keepdims=True), axis=1, keepdims=True)
             level = level + 1e-06
-            cache_ref[page, s, j] = (raw / level).astype(jnp.bfloat16)
+            cache_ref[page, j, s] = (raw / level).astype(jnp.bfloat16)
             scales_ref[page, s, j] = jnp.broadcast_to(level, (8, DH))
 
-    def pages(index, target):
-        return [
-            pltpu.make_async_remote_copy(
-                src_ref=ref.at[page],
-                dst_ref=ref.at[page],
-                send_sem=page_send.at[index, j],
-                recv_sem=page_recv.at[index, j],
-                device_id={"page": target},
-                device_id_type=MESH,
-            )
-            for j, ref in enumerate((cache_ref, scales_ref))
-        ]
-
-    def arrived(index):
-        origin = (page + n_page - index) % n_page
-        for j, ref in enumerate((cache_ref, scales_ref)):
-            pltpu.make_async_remote_copy(
-                src_ref=ref.at[origin],
-                dst_ref=ref.at[origin],
-                send_sem=page_send.at[index, j],
-                recv_sem=page_recv.at[index, j],
-                device_id={"page": (page + index) % n_page},
-                device_id_type=MESH,
-            ).wait_recv()
-
-    for d in range(1, chips):
+    reach = n_page // 2
+
+    def hop(k, j, way):
+        origin = (page + n_page - way * (k - 1)) % n_page
+        return pltpu.make_async_remote_copy(
+            src_ref=cache_ref.at[origin, j],
+            dst_ref=cache_ref.at[origin, j],
+            send_sem=page_send.at[k, j, (way + 1) // 2],
+            recv_sem=page_recv.at[k, j, (way + 1) // 2],
+            device_id={"page": (page + n_page + way) % n_page},
+            device_id_type=MESH,
+        )
+
+    def coming(k, j, way):
+        origin = (page + n_page - way * k) % n_page
+        return pltpu.make_async_remote_copy(
+            src_ref=cache_ref.at[origin, j],
+            dst_ref=cache_ref.at[origin, j],
+            send_sem=page_send.at[k, j, (way + 1) // 2],
+            recv_sem=page_recv.at[k, j, (way + 1) // 2],
+            device_id={"page": (page + n_page + way) % n_page},
+            device_id_type=MESH,
+        )
+
+    def used(k):
+        both = [(0, 1), (1, -1), (1, 1), (0, -1)]
+        return both[:2] if 2 * k == n_page else both
+
+    def send_hop(k):
+        for j, way in used(k):
+            if k > 1:
+                coming(k - 1, j, way).wait_recv()
+            copy = hop(k, j, way)
+            copy.start()
+            started.append(copy)
+
+    def levels(index, origin):
+        return pltpu.make_async_remote_copy(
+            src_ref=scales_ref.at[origin],
+            dst_ref=scales_ref.at[origin],
+            send_sem=level_send.at[index],
+            recv_sem=level_recv.at[index],
+            device_id={"page": (page + index) % n_page},
+            device_id_type=MESH,
+        )
+
+    for d in range(half, chips):
         attend = chunk(d, False)
-        if d == 1:
+        if d == half:
+            send_hop(1)
             for index in range(1, n_page):
-                for copy in pages(index, (page + index) % n_page):
-                    copy.start()
-                    started.append(copy)
+                copy = levels(index, page)
+                copy.start()
+                started.append(copy)
         attend()
+        if d == half:
+            for k in range(2, reach + 1):
+                send_hop(k)
 
     @pl.loop(0, groups)
     def _(g):
@@ -222,7 +264,12 @@
                 ] = (acc[g, i, lines, :DH] / acc[g, i, lines, DH:]).astype(jnp.bfloat16)
 
     for index in range(1, n_page):
-        arrived(index)
+        levels(index, (page + n_page - index) % n_page).wait_recv()
+    for k in range(1, reach + 1):
+        passed = used(k + 1) if k < reach else []
+        for j, way in used(k):
+            if (j, way) not in passed:
+                coming(k, j, way).wait_recv()
     for copy in started:
         copy.wait_send()
 
@@ -241,7 +288,7 @@
         functools.partial(kernel, n, n_page, heads),
         out_shape=(
             jax.ShapeDtypeStruct((rows, heads * DH), jnp.bfloat16),
-            jax.ShapeDtypeStruct((n_page, spans, 2, PAGE, DH), jnp.bfloat16),
+            jax.ShapeDtypeStruct((n_page, 2, spans, PAGE, DH), jnp.bfloat16),
             jax.ShapeDtypeStruct((n_page, spans, 2, 8, DH), jnp.float32),
         ),
         in_specs=[hbm] * 5,
@@ -259,8 +306,10 @@
             pltpu.SemaphoreType.DMA((n, 2)),
             pltpu.SemaphoreType.DMA((n, 2)),
             pltpu.SemaphoreType.DMA((5,)),
-            pltpu.SemaphoreType.DMA((n_page, 2)),
-            pltpu.SemaphoreType.DMA((n_page, 2)),
+            pltpu.SemaphoreType.DMA((n_page // 2 + 1, 2, 2)),
+            pltpu.SemaphoreType.DMA((n_page // 2 + 1, 2, 2)),
+            pltpu.SemaphoreType.DMA((n_page,)),
+            pltpu.SemaphoreType.DMA((n_page,)),
         ],
         compiler_params=pltpu.CompilerParams(
             collective_id=0, has_side_effects=True, vmem_limit_bytes=67043328
@@ -272,7 +321,7 @@
         keys.reshape(spans, SPAN, DH),
         values.reshape(spans, SPAN, DH),
     )
-    cache = cache.transpose(1, 0, 2, 3, 4)
+    cache = cache.transpose(2, 0, 1, 3, 4)
     scales = scales[:, :, :, 0, 0].transpose(1, 0, 2)
     return attended, cache, scales
 

time: 34.7 us -> 36.1 us (1.040)
  Pallas kernels: 29.4 us -> 30.7 us
    pallas_call x1, Pallas kernels: 29.4 us -> 30.7 us  [on_device(): pl.pallas_call(functools.partial(kernel, n, n_page, heads), out_shape=(ja...]
where the time goes in v3:
time: 36.1 us; the launch traced here: 35.8 us
  Pallas kernels  30.7 us (85%)
  local copies, waits for them, and re-layouts  4.47 us (12%)
  between operations  0.65 us (2%)
    pallas_call x1, Pallas kernels, on_device(): pl.pallas_call(functools.partial(kernel, n, n_page, heads), out_shape=(ja...  30.7 us
    unnamed x4, local copies, waits for them, and re-layouts  2.95 us
    slice x2, local copies, waits for them, and re-layouts, on_device(): scales = scales[:, :, :, 0, 0].transpose(1, 0, 2)  1.53 us

profile of v3, /device:TPU:1, one launch (start us, length us, event | category | flops | bytes accessed | tf_op | source)
XLA Modules:
  0.0 35.8 jit_solution(12574686711020771502)
XLA Ops:
  0.6 30.7 %shard_map.76 = (bf16[256,2048]{1,0:T(8,128)(2,1)}, bf16[4,2,2,128,128]{4,3,2,1,0:T(8,128)(2,1)}, f32[4,2,2,8,128]{4,3,2,1,0:T(8,128)}) custom-call(s32[16]{0:T(128)} %table_in.1, s32[16]{0:T(128)} %slots_in.1, bf16[256,2048]{1,0:T(8,128)(2,1)} %q_in.1, bf16[2,128,128]{2,1,0:T(8,128)(2,1)} %bitcast.7, bf16[2,128,128]{2,1,0:T(8,128)(2,1)} %bitcast.8), custom_call_target="tpu_custom_call" | custom-call | tf_op jit(solution)/shard_map/pallas_call | solution.py:287
  31.3 0.0 copy-start
  31.3 2.0 %copy.9 = bf16[2,4,2,128,128]{4,3,2,1,0:T(8,128)(2,1)} copy(bf16[2,4,2,128,128]{4,3,0,2,1:T(8,128)(2,1)} %bitcast.6) | data formatting | bytes 1048576
  33.3 0.8 %slice.3 = f32[4,2,2,1,1]{4,3,2,1,0:T(1,128)S(1)} slice(f32[4,2,2,8,128]{4,3,2,1,0:T(8,128)} %get-tuple-element.8), slice={[0:4], [0:2], [0:2], [0:1], [0:1]} | slice | bytes 128 | tf_op jit(solution)/shard_map/slice | solution.py:325
  34.1 0.7 %copy.8 = f32[4,2,2,1,1]{0,2,4,3,1:T(2,128)} copy(f32[4,2,2,1,1]{4,3,2,1,0:T(1,128)S(1)} %slice.3) | data formatting | bytes 128 | tf_op jit(solution)/shard_map/slice | solution.py:325
  34.8 0.0 copy-done
  34.8 1.0 %copy.11 = bf16[256,2048]{1,0:T(8,128)(2,1)} copy(bf16[256,2048]{1,0:T(8,128)(2,1)S(1)} %copy-done) | data formatting | bytes 2097152
Async XLA Ops:
  31.3 3.5 %copy-start = (bf16[256,2048]{1,0:T(8,128)(2,1)S(1)}, bf16[256,2048]{1,0:T(8,128)(2,1)}, u32[]{:S(2)}) copy-start(bf16[256,2048]{1,0:T(8,128)(2,1)} %get-tuple-element.15) | copy-start | bytes 3145732
